TPU v7x, 512 devices: a whole 4x8x8 slice. The times are simulated.
512 devices in a mesh: sta: 8 (over z_hi, x), tm: 64 (over y, z_lo, core).
Axes of the slice: x: 4, y: 8, z: 8 (z_hi: 2, z_lo: 4; z = z_hi * 4 + z_lo), core: 2. Of those that a mesh axis runs over, the one named last changes fastest.
Arguments:
- record: bfloat16 [96, 49152], P('sta', 'tm')
- templates: bfloat16 [64, 96, 512], P('tm', 'sta'), may hold values from -6 to 6
- shifts: int32 [96], P('sta'), may hold values from 0 to 255, as said below
- live_mask: int32 [96], P('sta'), may hold values 0 or 1
- plan: int32 [64], replicated, may hold values from 0 to 63, each once
Outputs:
- stacks: float32 [64, 49152], P('sta', 'tm')
Inputs may be any that keep to these rules, and one draw needn't show every extreme that they name: `shifts`: some channel has the shift 256 - 1. `plan`: each bank slot appears once.
All inputs are finite; a program needn't handle non-finite values. No bound on the sum of `live_mask` on one device may be relied on, other than what follows from the above.
Results may differ from a plain program's by a relative error of at most 0.0003.
Values may be sent and summed in bfloat16 or wider, within the bound.
A program may use at most 64 MiB of HBM per device.

v0:
```python
import math
import jax
import jax.numpy as jnp
from jax import lax
from jax.sharding import PartitionSpec as P

CHANNELS = 96


def passed_along(shard, axis, by):
    count = lax.axis_size(axis)
    pairs = [(i, i + by) for i in range(count) if 0 <= i + by < count]
    return lax.ppermute(shard, axis, pairs)


def hankel_rows(signal, taps_len, span_len):
    length = signal.shape[0]
    copies = jnp.tile(signal, taps_len + 1)
    skewed = copies[: taps_len * (length + 1)].reshape(taps_len, length + 1)
    return skewed[:, :span_len]


def correlate(panels_in, aligned, live_vals, taps_len, span_len, group_cap):
    tmpl_rows, chan_count, _ = panels_in.shape
    group_size = math.gcd(chan_count, group_cap)
    overall = math.sqrt(taps_len / CHANNELS)
    norm_vals = jnp.sqrt(jnp.sum(jnp.square(panels_in.astype(jnp.float32)), axis=2) + 1e-06)
    weights = live_vals[None, :] * overall / norm_vals
    in_pos = lax.broadcasted_iota(jnp.int32, (span_len + taps_len, span_len), 0)
    out_pos = lax.broadcasted_iota(jnp.int32, (span_len + taps_len, span_len), 1)
    band_ones = ((in_pos >= out_pos) & (in_pos < out_pos + taps_len)).astype(jnp.float32)

    def add_group(group_idx, running):
        first_chan = group_idx * group_size
        panel_part = lax.dynamic_slice_in_dim(panels_in, first_chan, group_size, 1)
        window = lax.dynamic_slice_in_dim(aligned, first_chan, group_size, 0)
        stacked = jax.vmap(lambda signal_row: hankel_rows(signal_row, taps_len, span_len))(window)
        products = jnp.einsum(
            "rgl,glt->rgt", panel_part, stacked, preferred_element_type=jnp.float32
        )
        squares = jnp.square(window.astype(jnp.float32))
        energy = jnp.dot(squares, band_ones, precision=lax.Precision.HIGHEST)
        weighting = lax.dynamic_slice_in_dim(weights, first_chan, group_size, 1)
        scaled = products * weighting[:, :, None] * lax.rsqrt(energy + 1e-06)[None, :, :]
        return running + jnp.sum(scaled, axis=1)

    start_val = jnp.zeros((tmpl_rows, span_len), jnp.float32)
    return lax.fori_loop(0, chan_count // group_size, add_group, start_val)


def per_device(record, templates, shifts, live_mask, plan):
    taps_len = templates.shape[2]
    span_len = record.shape[1]
    live_vals = live_mask.astype(jnp.float32)
    rim_part = passed_along(record, "tm", -1)
    extended = jnp.concatenate([record, rim_part], axis=1)
    aligned = jax.vmap(
        lambda signal_row, lag_val: lax.dynamic_slice_in_dim(
            signal_row, lag_val, span_len + taps_len
        )
    )(extended, shifts)
    bank_all = lax.all_gather(templates, "tm", axis=0, tiled=True)
    ordered = jnp.take(bank_all, plan, axis=0)
    partial_value = correlate(ordered, aligned, live_vals, taps_len, span_len, 8)
    return lax.psum_scatter(partial_value, "sta", scatter_dimension=0, tiled=True)


def solution(mesh):
    placed = (P("sta", "tm"), P("tm", "sta", None), P("sta"), P("sta"), P())
    return jax.shard_map(
        per_device, mesh=mesh, in_specs=placed, out_specs=P("sta", "tm"), check_vma=False
    )
```

profile of v0, /device:TPU:8, one launch (start us, length us, event | category | flops | bytes accessed | tf_op | source)
XLA Modules:
  0.0 318.2 jit_solution(1732965342201204)
XLA Ops:
  6.5 7.3 %collective-permute-start = (bf16[12,768]{1,0:T(8,128)(2,1)}, bf16[12,768]{1,0:T(8,128)(2,1)S(1)}, u32[]{:S(2)}, u32[]{:S(2)}) collective-permute-start(bf16[12,768]{1,0:T(8,128)(2,1)} %param.7), channel_id=1, source_target_pairs={{1,0},{2,1},{3,2},{4,3},{5,4},{6,5},{7,6},{8,7},{9,8},{10,9},{11,1... | collective-permute-start | bytes 55304 | tf_op jit(solution)/shard_map/ppermute | solution.py:13
  15.9 73.3 %all_gather.3 = bf16[64,12,512]{2,1,0:T(8,128)(2,1)S(1)} all-gather(bf16[1,12,512]{2,1,0:T(8,128)(2,1)} %param.8), channel_id=1, replica_groups=mesh['sta'=8,'tm'=64] {'tm'}, dimensions={0}, use_global_device_ids=true | all-gather | bytes 798720 | tf_op jit(solution)/shard_map/all_gather | solution.py:62
  91.1 25.1 %while.15 = (s32[]{:T(128)}, bf16[12,1536]{1,0:T(8,128)(2,1)S(1)}, s32[12,2]{0,1:T(2,128)S(1)}, bf16[12,1280]{1,0:T(8,128)(2,1)S(1)}, s32[]{:T(128)}, /*index=5*/s32[]{:T(128)}) while((s32[]{:T(128)}, bf16[12,1536]{1,0:T(8,128)(2,1)S(1)}, s32[12,2]{0,1:T(2,128)S(1)}, bf16[12,1280]{1,0:T(8,128)(2,1)S(1)}, s32[]{:T(128)}, /*index=5*/s32[]{:T(128)}) %tuple.49), condition=%wide.while_cond, body=%wide.while_body.sunk | while | flops 2 | bytes 10361 | solution.py:58
  91.8 1.4 dynamic-slice.7
  93.9 1.4 dynamic-slice.7
  96.0 1.4 dynamic-slice.7
  98.1 1.4 dynamic-slice.7
  100.1 1.4 dynamic-slice.7
  102.2 1.4 dynamic-slice.7
  104.3 1.4 dynamic-slice.7
  106.4 1.4 dynamic-slice.7
  108.5 1.4 dynamic-slice.7
  116.2 98.8 %while.16 = (s32[]{:T(128)}, f32[64,768]{1,0:T(8,128)S(1)}, bf16[12,1280]{1,0:T(8,128)(2,1)S(1)}, bf16[64,12,512]{2,1,0:T(8,128)(2,1)S(1)}, f32[64,12]{0,1:T(8,1...) while((s32[]{:T(128)}, f32[64,768]{1,0:T(8,128)S(1)}, ...), condition=%wide.region_3.4_spmd.clone, body=%wide.region_1.3_spmd.clone.sunk | while | flops 253096960 | bytes 52031664 | solution.py:48
  116.6 2.0 copy.16
  118.6 4.0 %slice.49 = bf16[4,655872]{1,0:T(4,128)(2,1)} slice(bf16[4,656640]{1,0:T(4,128)(2,1)S(1)} %bitcast.25), slice={[0:4], [0:655872]} | slice | bytes 10493952 | tf_op jit(solution)/shard_map/while/body/eval_jaxpr/vmap()/slice | solution.py:19
  122.6 6.8 %reshape.53 = bf16[2623488]{0:T(1024)(128)(2,1)} reshape(bf16[4,655872]{1,0:T(4,128)(2,1)} %slice.49) | data formatting | bytes 10493952 | tf_op jit(solution)/shard_map/while
  129.5 14.9 %reshape.54 = bf16[4,512,1281]{2,1,0:T(8,128)(2,1)} reshape(bf16[2623488]{0:T(1024)(128)(2,1)} %reshape.53) | data formatting | bytes 10493952 | tf_op jit(solution)/shard_map/while/body/eval_jaxpr/vmap()/reshape | solution.py:19
  144.4 2.0 fusion.44
  146.5 2.6 fusion.45
  149.5 2.0 copy.16
  151.6 4.0 %slice.49 = bf16[4,655872]{1,0:T(4,128)(2,1)} slice(bf16[4,656640]{1,0:T(4,128)(2,1)S(1)} %bitcast.25), slice={[0:4], [0:655872]} | slice | bytes 10493952 | tf_op jit(solution)/shard_map/while/body/eval_jaxpr/vmap()/slice | solution.py:19
  155.6 6.8 %reshape.53 = bf16[2623488]{0:T(1024)(128)(2,1)} reshape(bf16[4,655872]{1,0:T(4,128)(2,1)} %slice.49) | data formatting | bytes 10493952 | tf_op jit(solution)/shard_map/while
  162.4 14.9 %reshape.54 = bf16[4,512,1281]{2,1,0:T(8,128)(2,1)} reshape(bf16[2623488]{0:T(1024)(128)(2,1)} %reshape.53) | data formatting | bytes 10493952 | tf_op jit(solution)/shard_map/while/body/eval_jaxpr/vmap()/reshape | solution.py:19
  177.3 2.0 fusion.44
  179.5 2.6 fusion.45
  182.5 2.0 copy.16
  184.5 4.0 %slice.49 = bf16[4,655872]{1,0:T(4,128)(2,1)} slice(bf16[4,656640]{1,0:T(4,128)(2,1)S(1)} %bitcast.25), slice={[0:4], [0:655872]} | slice | bytes 10493952 | tf_op jit(solution)/shard_map/while/body/eval_jaxpr/vmap()/slice | solution.py:19
  188.5 6.8 %reshape.53 = bf16[2623488]{0:T(1024)(128)(2,1)} reshape(bf16[4,655872]{1,0:T(4,128)(2,1)} %slice.49) | data formatting | bytes 10493952 | tf_op jit(solution)/shard_map/while
  195.4 14.9 %reshape.54 = bf16[4,512,1281]{2,1,0:T(8,128)(2,1)} reshape(bf16[2623488]{0:T(1024)(128)(2,1)} %reshape.53) | data formatting | bytes 10493952 | tf_op jit(solution)/shard_map/while/body/eval_jaxpr/vmap()/reshape | solution.py:19
  210.3 2.0 fusion.44
  212.4 2.6 fusion.45
  215.7 95.6 %reduce-scatter.2.cloned.1.call-done = f32[8,768]{1,0:T(8,128)} async-done(((f32[64,768]{1,0:T(8,128)}), f32[8,768]{1,0:T(8,128)}) %reduce-scatter.2.cloned.1.call-update) | async-done | bytes 24592 | tf_op jit(solution)/shard_map/reduce_scatter | solution.py:65
  (76 shorter events, 18.9 us)
Async XLA Ops:
  6.5 84.6 %copy-start.1 = (bf16[12,768]{1,0:T(8,128)(2,1)S(1)}, bf16[12,768]{1,0:T(8,128)(2,1)}, u32[]{:S(2)}) copy-start(bf16[12,768]{1,0:T(8,128)(2,1)} %param.7) | copy-start | bytes 55300
  6.5 304.8 %reduce-scatter.2.cloned.1.call-start = ((), (), s32[]{:S(2)}) async-start(), calls=%async_computation.1 | async-start | bytes 221184 | tf_op jit(solution)/shard_map/reduce_scatter | solution.py:65
  6.5 84.6 %collective-permute-start = (bf16[12,768]{1,0:T(8,128)(2,1)}, bf16[12,768]{1,0:T(8,128)(2,1)S(1)}, u32[]{:S(2)}, u32[]{:S(2)}) collective-permute-start(bf16[12,768]{1,0:T(8,128)(2,1)} %param.7), channel_id=1, source_target_pairs={{1,0},{2,1},{3,2},{4,3},{5,4},{6,5},{7,6},{8,7},{9,8},{10,9},{11,1... | collective-permute-start | bytes 55304 | tf_op jit(solution)/shard_map/ppermute | solution.py:13
  215.0 0.7 copy-start
Sparse Core Ops, SparseCore 0:
  215.9 95.4 reduce-scatter.1
where the time goes:
time: 319 us; the launch traced here: 318 us
  local copies, waits for them, and re-layouts  111 us (35%)
  waiting for transfers between devices  95.6 us (30%)
  blocking collectives  73.3 us (23%)
  matrix products  13.6 us (4%)
  between operations  13.5 us (4%)
  starting transfers between devices  7.34 us (2%)
  other arithmetic  3.33 us (1%)
    reduce_scatter x1, waiting for transfers between devices, per_device(): lax.psum_scatter(partial_value, 'sta', scatter_dimension=0, tiled=True)  95.6 us
    all_gather x1, blocking collectives, per_device(): bank_all = lax.all_gather(templates, 'tm', axis=0, tiled=True)  73.3 us
    reshape x3, local copies, waits for them, and re-layouts, hankel_rows(): skewed = copies[:taps_len * (length + 1)].reshape(taps_len, length + 1)  44.7 us
    while x9, local copies, waits for them, and re-layouts  27.6 us
    gather x48, local copies, waits for them, and re-layouts  24.8 us
    slice x3, local copies, waits for them, and re-layouts, hankel_rows(): skewed = copies[:taps_len * (length + 1)].reshape(taps_len, length + 1)  12 us
    dot_general x3, matrix products, add_group(): jnp.einsum('rgl,glt->rgt', panel_part, stacked, preferred_element_type=jn...  7.72 us
    ppermute x1, starting transfers between devices, passed_along(): return lax.ppermute(shard, axis, pairs)  7.34 us
  transfers between devices with their start and end apart: 2, of which 1 were waited for; matrix products, arithmetic and copies ran while one was open for 1% of the time, Pallas kernels for 0%

commit v1 on v0

--- a/solution.py
+++ b/solution.py
@@ -59,7 +59,9 @@
             signal_row, lag_val, span_len + taps_len
         )
     )(extended, shifts)
-    bank_all = lax.all_gather(templates, "tm", axis=0, tiled=True)
+    response = jnp.stack([templates] * lax.axis_size("tm"))
+    aux = lax.all_to_all(response, "tm", split_axis=0, concat_axis=0)
+    bank_all = jnp.concatenate(aux, axis=0)
     ordered = jnp.take(bank_all, plan, axis=0)
     partial_value = correlate(ordered, aligned, live_vals, taps_len, span_len, 8)
     return lax.psum_scatter(partial_value, "sta", scatter_dimension=0, tiled=True)

time: 319 us -> 252 us (0.79)
  blocking collectives: 73.3 us -> 0 us
  starting transfers between devices: 7.34 us -> 15.6 us
  waiting for transfers between devices: 95.6 us -> 91.3 us
    all_gather x1 -> x0, blocking collectives: 73.3 us -> none  [per_device(): bank_all = lax.all_gather(templates, 'tm', axis=0, tiled=True)]
    all_to_all x0 -> x1, starting transfers between devices: none -> 8.33 us  [per_device(): aux = lax.all_to_all(response, 'tm', split_axis=0, concat_axis=0)]
    reduce_scatter x1, waiting for transfers between devices: 95.6 us -> 91.2 us  [per_device(): lax.psum_scatter(partial_value, 'sta', scatter_dimension=0, tiled=True)]
  transfers between devices with their start and end apart: 2 -> 3, of which waited for: 1 -> 2; matrix products, arithmetic and copies ran while one was open for 1% -> 12% of each run, Pallas kernels for 0% -> 0%
where the time goes in v1:
time: 252 us; the launch traced here: 251 us
  local copies, waits for them, and re-layouts  112 us (44%)
  waiting for transfers between devices  91.3 us (36%)
  starting transfers between devices  15.6 us (6%)
  matrix products  13.6 us (5%)
  between operations  13.5 us (5%)
  other arithmetic  4.06 us (2%)
    reduce_scatter x1, waiting for transfers between devices, per_device(): lax.psum_scatter(partial_value, 'sta', scatter_dimension=0, tiled=True)  91.2 us
    reshape x3, local copies, waits for them, and re-layouts, hankel_rows(): skewed = copies[:taps_len * (length + 1)].reshape(taps_len, length + 1)  44.7 us
    while x9, local copies, waits for them, and re-layouts  27.6 us
    gather x48, local copies, waits for them, and re-layouts  24 us
    slice x3, local copies, waits for them, and re-layouts, hankel_rows(): skewed = copies[:taps_len * (length + 1)].reshape(taps_len, length + 1)  12.1 us
    all_to_all x1, starting transfers between devices, per_device(): aux = lax.all_to_all(response, 'tm', split_axis=0, concat_axis=0)  8.33 us
    dot_general x3, matrix products, add_group(): jnp.einsum('rgl,glt->rgt', panel_part, stacked, preferred_element_type=jn...  7.72 us
    ppermute x1, starting transfers between devices, passed_along(): return lax.ppermute(shard, axis, pairs)  7.21 us
  transfers between devices with their start and end apart: 3, of which 2 were waited for; matrix products, arithmetic and copies ran while one was open for 12% of the time, Pallas kernels for 0%

profile of v1, /device:TPU:8, one launch (start us, length us, event | category | flops | bytes accessed | tf_op | source)
XLA Modules:
  0.0 250.8 jit_solution(2806785707973988296)
XLA Ops:
  6.5 7.2 %collective-permute-start = (bf16[12,768]{1,0:T(8,128)(2,1)}, bf16[12,768]{1,0:T(8,128)(2,1)S(1)}, u32[]{:S(2)}, u32[]{:S(2)}) collective-permute-start(bf16[12,768]{1,0:T(8,128)(2,1)} %param.7), channel_id=1, source_target_pairs={{1,0},{2,1},{3,2},{4,3},{5,4},{6,5},{7,6},{8,7},{9,8},{10,9},{11,1... | collective-permute-start | bytes 55304 | tf_op jit(solution)/shard_map/ppermute | solution.py:13
  13.8 1.8 stack.2
  15.6 8.3 %all-to-all-start = ((bf16[64,1,12,512]{3,2,1,0:T(8,128)(2,1)}), bf16[64,1,12,512]{3,2,1,0:T(8,128)(2,1)S(1)}, u32[]{:S(2)}, u32[]{:S(2)}) async-start(bf16[64,1,12,512]{3,2,1,0:T(8,128)(2,1)} %stack.2), calls=%async_computation | async-start | bytes 2097152 | tf_op jit(solution)/shard_map/all_to_all | solution.py:63
  27.4 24.3 %while.15 = (s32[]{:T(128)}, bf16[12,1536]{1,0:T(8,128)(2,1)S(1)}, s32[12,2]{0,1:T(2,128)S(1)}, bf16[12,1280]{1,0:T(8,128)(2,1)S(1)}, s32[]{:T(128)}, /*index=5*/s32[]{:T(128)}) while((s32[]{:T(128)}, bf16[12,1536]{1,0:T(8,128)(2,1)S(1)}, s32[12,2]{0,1:T(2,128)S(1)}, bf16[12,1280]{1,0:T(8,128)(2,1)S(1)}, s32[]{:T(128)}, /*index=5*/s32[]{:T(128)}) %tuple.49), condition=%wide.while_cond, body=%wide.while_body.sunk | while | flops 2 | bytes 10361 | solution.py:58
  28.1 1.3 dynamic-slice.7
  30.1 1.3 dynamic-slice.7
  32.1 1.3 dynamic-slice.7
  34.1 1.3 dynamic-slice.7
  36.2 1.3 dynamic-slice.7
  38.2 1.3 dynamic-slice.7
  40.2 1.3 dynamic-slice.7
  48.3 1.3 dynamic-slice.7
  53.0 99.0 %while.16 = (s32[]{:T(128)}, f32[64,768]{1,0:T(8,128)S(1)}, bf16[12,1280]{1,0:T(8,128)(2,1)S(1)}, bf16[64,12,512]{2,1,0:T(8,128)(2,1)S(1)}, f32[64,12]{0,1:T(8,1...) while((s32[]{:T(128)}, f32[64,768]{1,0:T(8,128)S(1)}, ...), condition=%wide.region_3.4_spmd.clone, body=%wide.region_1.3_spmd.clone.sunk | while | flops 253096960 | bytes 52031664 | solution.py:48
  53.4 2.0 copy.16
  55.4 4.0 %slice.49 = bf16[4,655872]{1,0:T(4,128)(2,1)} slice(bf16[4,656640]{1,0:T(4,128)(2,1)S(1)} %bitcast.27), slice={[0:4], [0:655872]} | slice | bytes 10493952 | tf_op jit(solution)/shard_map/while/body/eval_jaxpr/vmap()/slice | solution.py:19
  59.5 6.8 %reshape.60 = bf16[2623488]{0:T(1024)(128)(2,1)} reshape(bf16[4,655872]{1,0:T(4,128)(2,1)} %slice.49) | data formatting | bytes 10493952 | tf_op jit(solution)/shard_map/while
  66.3 14.9 %reshape.61 = bf16[4,512,1281]{2,1,0:T(8,128)(2,1)} reshape(bf16[2623488]{0:T(1024)(128)(2,1)} %reshape.60) | data formatting | bytes 10493952 | tf_op jit(solution)/shard_map/while/body/eval_jaxpr/vmap()/reshape | solution.py:19
  81.2 2.0 fusion.44
  83.4 2.6 %fusion.45 = f32[64,768]{1,0:T(8,128)S(1)} fusion(bf16[4,512,1281]{2,1,0:T(8,128)(2,1)} %reshape.61, f32[4,768]{1,0:T(4,128)S(1)} %fusion.44, f32[64,4]{0,1:T(4,128)S(1)} %constant_dynamic-slice_fusion.10, bf16[64,4,512]{2,1,0:T(4,128)(2,1)S(1)} %constant_dynamic-slice_fusion.11), kind=kOutput, calls=%fused_computation.15.clone.1 | convolution fusion | flops 201867264 | bytes 3617792 | tf_op jit(solution)/shard_map/while/body/eval_jaxpr/rgl,glt->rgt/dot_general | solution.py:38
  86.4 2.0 copy.16
  88.4 4.0 %slice.49 = bf16[4,655872]{1,0:T(4,128)(2,1)} slice(bf16[4,656640]{1,0:T(4,128)(2,1)S(1)} %bitcast.27), slice={[0:4], [0:655872]} | slice | bytes 10493952 | tf_op jit(solution)/shard_map/while/body/eval_jaxpr/vmap()/slice | solution.py:19
  92.5 6.8 %reshape.60 = bf16[2623488]{0:T(1024)(128)(2,1)} reshape(bf16[4,655872]{1,0:T(4,128)(2,1)} %slice.49) | data formatting | bytes 10493952 | tf_op jit(solution)/shard_map/while
  99.3 14.9 %reshape.61 = bf16[4,512,1281]{2,1,0:T(8,128)(2,1)} reshape(bf16[2623488]{0:T(1024)(128)(2,1)} %reshape.60) | data formatting | bytes 10493952 | tf_op jit(solution)/shard_map/while/body/eval_jaxpr/vmap()/reshape | solution.py:19
  114.2 2.0 fusion.44
  116.4 2.6 %fusion.45 = f32[64,768]{1,0:T(8,128)S(1)} fusion(bf16[4,512,1281]{2,1,0:T(8,128)(2,1)} %reshape.61, f32[4,768]{1,0:T(4,128)S(1)} %fusion.44, f32[64,4]{0,1:T(4,128)S(1)} %constant_dynamic-slice_fusion.10, bf16[64,4,512]{2,1,0:T(4,128)(2,1)S(1)} %constant_dynamic-slice_fusion.11), kind=kOutput, calls=%fused_computation.15.clone.1 | convolution fusion | flops 201867264 | bytes 3617792 | tf_op jit(solution)/shard_map/while/body/eval_jaxpr/rgl,glt->rgt/dot_general | solution.py:38
  119.4 2.0 copy.16
  121.4 4.0 %slice.49 = bf16[4,655872]{1,0:T(4,128)(2,1)} slice(bf16[4,656640]{1,0:T(4,128)(2,1)S(1)} %bitcast.27), slice={[0:4], [0:655872]} | slice | bytes 10493952 | tf_op jit(solution)/shard_map/while/body/eval_jaxpr/vmap()/slice | solution.py:19
  125.5 6.8 %reshape.60 = bf16[2623488]{0:T(1024)(128)(2,1)} reshape(bf16[4,655872]{1,0:T(4,128)(2,1)} %slice.49) | data formatting | bytes 10493952 | tf_op jit(solution)/shard_map/while
  132.3 14.9 %reshape.61 = bf16[4,512,1281]{2,1,0:T(8,128)(2,1)} reshape(bf16[2623488]{0:T(1024)(128)(2,1)} %reshape.60) | data formatting | bytes 10493952 | tf_op jit(solution)/shard_map/while/body/eval_jaxpr/vmap()/reshape | solution.py:19
  147.2 2.0 fusion.44
  149.4 2.6 %fusion.45 = f32[64,768]{1,0:T(8,128)S(1)} fusion(bf16[4,512,1281]{2,1,0:T(8,128)(2,1)} %reshape.61, f32[4,768]{1,0:T(4,128)S(1)} %fusion.44, f32[64,4]{0,1:T(4,128)S(1)} %constant_dynamic-slice_fusion.10, bf16[64,4,512]{2,1,0:T(4,128)(2,1)S(1)} %constant_dynamic-slice_fusion.11), kind=kOutput, calls=%fused_computation.15.clone.1 | convolution fusion | flops 201867264 | bytes 3617792 | tf_op jit(solution)/shard_map/while/body/eval_jaxpr/rgl,glt->rgt/dot_general | solution.py:38
  152.7 91.2 %reduce-scatter.2.cloned.1.call-done = f32[8,768]{1,0:T(8,128)} async-done(((f32[64,768]{1,0:T(8,128)}), f32[8,768]{1,0:T(8,128)}) %reduce-scatter.2.cloned.1.call-update) | async-done | bytes 24592 | tf_op jit(solution)/shard_map/reduce_scatter | solution.py:67
  (76 shorter events, 20.9 us)
Async XLA Ops:
  6.5 20.1 %collective-permute-start = (bf16[12,768]{1,0:T(8,128)(2,1)}, bf16[12,768]{1,0:T(8,128)(2,1)S(1)}, u32[]{:S(2)}, u32[]{:S(2)}) collective-permute-start(bf16[12,768]{1,0:T(8,128)(2,1)} %param.7), channel_id=1, source_target_pairs={{1,0},{2,1},{3,2},{4,3},{5,4},{6,5},{7,6},{8,7},{9,8},{10,9},{11,1... | collective-permute-start | bytes 55304 | tf_op jit(solution)/shard_map/ppermute | solution.py:13
  15.6 36.2 %all-to-all-start = ((bf16[64,1,12,512]{3,2,1,0:T(8,128)(2,1)}), bf16[64,1,12,512]{3,2,1,0:T(8,128)(2,1)S(1)}, u32[]{:S(2)}, u32[]{:S(2)}) async-start(bf16[64,1,12,512]{3,2,1,0:T(8,128)(2,1)} %stack.2), calls=%async_computation | async-start | bytes 2097152 | tf_op jit(solution)/shard_map/all_to_all | solution.py:63
  23.9 220.0 %reduce-scatter.2.cloned.1.call-start = ((), (), s32[]{:S(2)}) async-start(), calls=%async_computation.2 | async-start | bytes 221184 | tf_op jit(solution)/shard_map/reduce_scatter | solution.py:67
  152.0 0.7 copy-start
Sparse Core Ops, SparseCore 0:
  152.8 91.0 reduce-scatter.1
